TPU v7x, 512 devices: a whole 4x4x16 slice. The times are simulated.
512 devices in a mesh: segment: 4 (over y), shard: 16 (over z), stream: 8 (over x, core).
Axes of the slice: x: 4, y: 4, z: 16, core: 2. Of those that a mesh axis runs over, the one named last changes fastest.
Arguments:
- latents: bfloat16 [32, 16, 16, 32, 256], P('stream', 'shard'), parts along dimension 0, may hold values from -6 to 6
- norm_gain: float32 [4, 256], P('segment'), may hold values from 0.25 to 1.75
- time_weight: bfloat16 [4, 3, 256, 256], P('segment'), may hold values from -0.21875 to 0.21875
- space_weight: bfloat16 [4, 9, 256, 256], P('segment'), may hold values from -0.125 to 0.125
- carry_in: bfloat16 [4, 16, 16, 32, 256], P('segment', 'stream', 'shard'), parts along dimension 1, may hold values from -6 to 6
Outputs:
- decoded: bfloat16 [32, 16, 16, 32, 256], P(('stream', 'segment'), 'shard'), parts along dimension 0
- carry_out: bfloat16 [4, 16, 16, 32, 256], P('segment', 'stream', 'shard'), parts along dimension 1
There are 8 independent parts, one for each index of `stream`. A program takes and returns all parts, laid end to end along the dimension named above; an argument that names none is the same for every part. Nothing has to cross between parts.
All inputs are finite; a program needn't handle non-finite values.
Results may differ from a plain program's by a relative error of at most 0.009.
Values may be sent and summed in bfloat16 or wider, within the bound.
No kernel may reach another device: no remote copies, remote signals or barrier semaphores. Data moves between devices by JAX's collectives and lax.ppermute only.
A program may use at most 64 MiB of HBM per device.

v0:
```python
import jax
import jax.numpy as jnp
from jax import lax
from jax.sharding import PartitionSpec as P


def shifted(block, axis, distance):
    devices = range(lax.axis_size(axis))
    route = [(i - distance, i) for i in devices if i - distance in devices]
    return lax.ppermute(block, axis, route)


def normalize(frames_in, gain_row):
    values = frames_in.astype(jnp.float32)
    inverse = lax.rsqrt(jnp.mean(values * values, axis=-1, keepdims=True) + 1e-06)
    return (values * inverse * gain_row).astype(jnp.bfloat16)


def project(frames_in, matrix):
    channels = frames_in.shape[-1]
    product = jnp.dot(frames_in.reshape(-1, channels), matrix, preferred_element_type=jnp.float32)
    return product.reshape(frames_in.shape[:-1] + (matrix.shape[1],))


def spatial(hidden, kernel):
    padded = jnp.pad(hidden, ((0, 0), (1, 1), (1, 1), (0, 0)))
    height = hidden.shape[1]
    across = hidden.shape[2]
    summed = jnp.zeros(hidden.shape, jnp.float32)
    for offset in range(9):
        row_shift = offset // 3
        col_shift = offset % 3
        summed = summed + project(
            padded[:, row_shift : row_shift + height, col_shift : col_shift + across],
            kernel[offset],
        )
    return summed


def body(latents, norm_gain, time_weight, space_weight, carry_in):
    sections = lax.axis_size("segment")
    segment_pos = lax.axis_index("segment")
    block_count = latents.shape[0]
    rounds = block_count + sections - 1
    gain_row = norm_gain[0]
    taps = time_weight[0]
    kernel = space_weight[0]
    frame_shape = latents.shape[1:]
    earlier = carry_in[0]
    arriving = jnp.zeros(frame_shape, jnp.bfloat16)
    finished = []
    for turn in range(rounds):
        if turn < block_count:
            fresh = latents[turn]
        else:
            fresh = jnp.zeros(frame_shape, jnp.bfloat16)
        current = jnp.where(segment_pos == 0, fresh, arriving)
        active = jnp.logical_and(turn - segment_pos >= 0, turn - segment_pos < block_count)
        normed = normalize(current, gain_row)
        by_rows = lax.all_to_all(normed, "shard", split_axis=1, concat_axis=0, tiled=True)
        frame_count = by_rows.shape[0]
        extended = jnp.concatenate([earlier, by_rows], axis=0)
        mixed = project(extended[0:frame_count], taps[0])
        mixed = mixed + project(extended[1 : frame_count + 1], taps[1])
        mixed = mixed + project(extended[2 : frame_count + 2], taps[2])
        row_hidden = jax.nn.silu(mixed).astype(jnp.bfloat16)
        earlier = jnp.where(active, by_rows[frame_count - 2 :], earlier)
        hidden = lax.all_to_all(row_hidden, "shard", split_axis=0, concat_axis=1, tiled=True)
        result = (current.astype(jnp.float32) + spatial(hidden, kernel)).astype(jnp.bfloat16)
        if turn >= sections - 1:
            finished.append(result)
        if turn + 1 < rounds:
            arriving = shifted(result, "segment", 1)
    stacked = jnp.stack(finished)
    delivered = lax.all_to_all(stacked, "segment", split_axis=0, concat_axis=0, tiled=True)
    per_segment = block_count // sections
    decoded = delivered[(sections - 1) * per_segment :]
    carry_out = earlier[None]
    return (decoded, carry_out)


def solution(mesh):
    placed = (
        P("stream", "shard", None, None, None),
        P("segment", None),
        P("segment", None, None, None),
        P("segment", None, None, None),
        P("segment", "stream", "shard", None, None),
    )
    return jax.shard_map(
        body,
        mesh=mesh,
        in_specs=placed,
        out_specs=(
            P(("stream", "segment"), "shard", None, None, None),
            P("segment", "stream", "shard", None, None),
        ),
        check_vma=False,
    )
```

profile of v0, /device:TPU:38, one launch (start us, length us, event | category | flops | bytes accessed | tf_op | source)
XLA Modules:
  0.0 432.6 jit_solution(15415007599045715710)
XLA Ops:
  0.7 1.1 fusion.24
  2.9 32.9 %all_to_all.173 = bf16[1,16,32,256]{3,2,0,1:T(8,128)(2,1)S(1)} all-to-all(bf16[1,16,32,256]{3,2,0,1:T(8,128)(2,1)S(1)} %fusion.205), channel_id=1, replica_groups=mesh['segment'=4,'shard'=16,'stream'=8] {'shard'}, dimensions={1} | all-to-all | bytes 524288 | tf_op jit(solution)/shard_map/all_to_all | solution.py:60
  36.7 23.7 %all_to_all.174 = bf16[16,1,32,256]{3,2,1,0:T(8,128)(2,1)S(1)} all-to-all(bf16[16,1,32,256]{3,2,1,0:T(8,128)(2,1)S(1)} %fusion.51), channel_id=1, replica_groups=mesh['segment'=4,'shard'=16,'stream'=8] {'shard'}, dimensions={0} | all-to-all | bytes 524288 | tf_op jit(solution)/shard_map/all_to_all | solution.py:68
  63.3 3.5 collective-permute-start
  66.8 5.0 %collective-permute-done = bf16[1,16,32,256]{3,2,1,0:T(8,128)(2,1)S(1)} collective-permute-done((bf16[1,16,32,256]{3,2,1,0:T(8,128)(2,1)S(1)}, bf16[1,16,32,256]{3,2,1,0:T(8,128)(2,1)S(1)}, u32[]{:S(2)}, u32[]{:S(2)}) %collective-permute-start) | collective-permute-done | bytes 262176 | tf_op jit(solution)/shard_map/ppermute | solution.py:10
  72.8 7.0 %all-to-all-start.2 = ((bf16[1,16,32,256]{3,2,0,1:T(8,128)(2,1)}), bf16[1,16,32,256]{3,2,0,1:T(8,128)(2,1)S(1)}, u32[]{:S(2)}, u32[]{:S(2)}) async-start(bf16[1,16,32,256]{3,2,0,1:T(8,128)(2,1)} %fusion.204), calls=%async_computation.2 | async-start | bytes 524288 | tf_op jit(solution)/shard_map/all_to_all | solution.py:60
  79.8 17.6 %all-to-all-done.2 = bf16[1,16,32,256]{3,2,0,1:T(8,128)(2,1)S(1)} async-done(((bf16[1,16,32,256]{3,2,0,1:T(8,128)(2,1)}), bf16[1,16,32,256]{3,2,0,1:T(8,128)(2,1)S(1)}, u32[]{:S(2)}, u32[]{:S(2)}) %all-to-all-start.2) | async-done | bytes 262176 | tf_op jit(solution)/shard_map/all_to_all | solution.py:60
  98.2 23.3 %all_to_all.175 = bf16[16,1,32,256]{3,2,1,0:T(8,128)(2,1)S(1)} all-to-all(bf16[16,1,32,256]{3,2,1,0:T(8,128)(2,1)S(1)} %fusion.50), channel_id=1, replica_groups=mesh['segment'=4,'shard'=16,'stream'=8] {'shard'}, dimensions={0} | all-to-all | bytes 524288 | tf_op jit(solution)/shard_map/all_to_all | solution.py:68
  123.7 4.4 %collective-permute-start.1 = (bf16[1,16,32,256]{3,2,1,0:T(8,128)(2,1)S(1)}, bf16[1,16,32,256]{3,2,1,0:T(8,128)(2,1)S(1)}, u32[]{:S(2)}, u32[]{:S(2)}) collective-permute-start(bf16[1,16,32,256]{3,2,1,0:T(8,128)(2,1)S(1)} %fusion.18), channel_id=1, source_target_pairs={{0,128},{128,256},{256,384},{1,129},{129,257},{257,385},{2,130},{1... | collective-permute-start | bytes 786440 | tf_op jit(solution)/shard_map/ppermute | solution.py:10
  128.1 3.9 collective-permute-done.1
  132.2 22.7 %all_to_all.176 = bf16[1,16,32,256]{3,2,0,1:T(8,128)(2,1)S(1)} all-to-all(bf16[1,16,32,256]{3,2,0,1:T(8,128)(2,1)S(1)} %fusion.203), channel_id=1, replica_groups=mesh['segment'=4,'shard'=16,'stream'=8] {'shard'}, dimensions={1} | all-to-all | bytes 524288 | tf_op jit(solution)/shard_map/all_to_all | solution.py:60
  155.7 22.5 %all_to_all.177 = bf16[16,1,32,256]{3,2,1,0:T(8,128)(2,1)S(1)} all-to-all(bf16[16,1,32,256]{3,2,1,0:T(8,128)(2,1)S(1)} %fusion.49), channel_id=1, replica_groups=mesh['segment'=4,'shard'=16,'stream'=8] {'shard'}, dimensions={0} | all-to-all | bytes 524288 | tf_op jit(solution)/shard_map/all_to_all | solution.py:68
  180.3 4.4 %collective-permute-start.2 = (bf16[1,16,32,256]{3,2,1,0:T(8,128)(2,1)S(1)}, bf16[1,16,32,256]{3,2,1,0:T(8,128)(2,1)S(1)}, u32[]{:S(2)}, u32[]{:S(2)}) collective-permute-start(bf16[1,16,32,256]{3,2,1,0:T(8,128)(2,1)S(1)} %fusion.17), channel_id=1, source_target_pairs={{0,128},{128,256},{256,384},{1,129},{129,257},{257,385},{2,130},{1... | collective-permute-start | bytes 786440 | tf_op jit(solution)/shard_map/ppermute | solution.py:10
  184.7 4.5 %collective-permute-done.2 = bf16[1,16,32,256]{3,2,1,0:T(8,128)(2,1)S(1)} collective-permute-done((bf16[1,16,32,256]{3,2,1,0:T(8,128)(2,1)S(1)}, bf16[1,16,32,256]{3,2,1,0:T(8,128)(2,1)S(1)}, u32[]{:S(2)}, u32[]{:S(2)}) %collective-permute-start.2) | collective-permute-done | bytes 262176 | tf_op jit(solution)/shard_map/ppermute | solution.py:10
  191.0 6.2 %all-to-all-start.6 = ((bf16[1,16,32,256]{3,2,0,1:T(8,128)(2,1)}), bf16[1,16,32,256]{3,2,0,1:T(8,128)(2,1)S(1)}, u32[]{:S(2)}, u32[]{:S(2)}) async-start(bf16[1,16,32,256]{3,2,0,1:T(8,128)(2,1)} %fusion.202), calls=%async_computation.6 | async-start | bytes 524288 | tf_op jit(solution)/shard_map/all_to_all | solution.py:60
  197.2 17.7 %all-to-all-done.6 = bf16[1,16,32,256]{3,2,0,1:T(8,128)(2,1)S(1)} async-done(((bf16[1,16,32,256]{3,2,0,1:T(8,128)(2,1)}), bf16[1,16,32,256]{3,2,0,1:T(8,128)(2,1)S(1)}, u32[]{:S(2)}, u32[]{:S(2)}) %all-to-all-start.6) | async-done | bytes 262176 | tf_op jit(solution)/shard_map/all_to_all | solution.py:60
  215.7 22.5 %all_to_all.178 = bf16[16,1,32,256]{3,2,1,0:T(8,128)(2,1)S(1)} all-to-all(bf16[16,1,32,256]{3,2,1,0:T(8,128)(2,1)S(1)} %fusion.48), channel_id=1, replica_groups=mesh['segment'=4,'shard'=16,'stream'=8] {'shard'}, dimensions={0} | all-to-all | bytes 524288 | tf_op jit(solution)/shard_map/all_to_all | solution.py:68
  240.8 4.5 %collective-permute-start.3 = (bf16[1,16,32,256]{3,2,1,0:T(8,128)(2,1)S(1)}, bf16[1,16,32,256]{3,2,1,0:T(8,128)(2,1)S(1)}, u32[]{:S(2)}, u32[]{:S(2)}) collective-permute-start(bf16[1,16,32,256]{3,2,1,0:T(8,128)(2,1)S(1)} %fusion.16), channel_id=1, source_target_pairs={{0,128},{128,256},{256,384},{1,129},{129,257},{257,385},{2,130},{1... | collective-permute-start | bytes 786440 | tf_op jit(solution)/shard_map/ppermute | solution.py:10
  245.3 3.9 collective-permute-done.3
  249.5 21.6 %all_to_all.179 = bf16[1,16,32,256]{3,2,0,1:T(8,128)(2,1)S(1)} all-to-all(bf16[1,16,32,256]{3,2,0,1:T(8,128)(2,1)S(1)} %fusion.201), channel_id=1, replica_groups=mesh['segment'=4,'shard'=16,'stream'=8] {'shard'}, dimensions={1} | all-to-all | bytes 524288 | tf_op jit(solution)/shard_map/all_to_all | solution.py:60
  272.0 22.3 %all_to_all.180 = bf16[16,1,32,256]{3,2,1,0:T(8,128)(2,1)S(1)} all-to-all(bf16[16,1,32,256]{3,2,1,0:T(8,128)(2,1)S(1)} %fusion.47), channel_id=1, replica_groups=mesh['segment'=4,'shard'=16,'stream'=8] {'shard'}, dimensions={0} | all-to-all | bytes 524288 | tf_op jit(solution)/shard_map/all_to_all | solution.py:68
  296.4 4.5 %collective-permute-start.4 = (bf16[1,16,32,256]{3,2,1,0:T(8,128)(2,1)S(1)}, bf16[1,16,32,256]{3,2,1,0:T(8,128)(2,1)S(1)}, u32[]{:S(2)}, u32[]{:S(2)}) collective-permute-start(bf16[1,16,32,256]{3,2,1,0:T(8,128)(2,1)S(1)} %fusion.15), channel_id=1, source_target_pairs={{0,128},{128,256},{256,384},{1,129},{129,257},{257,385},{2,130},{1... | collective-permute-start | bytes 786440 | tf_op jit(solution)/shard_map/ppermute | solution.py:10
  300.9 3.9 collective-permute-done.4
  305.8 6.0 %all-to-all-start.10 = ((bf16[1,16,32,256]{3,2,0,1:T(8,128)(2,1)}), bf16[1,16,32,256]{3,2,0,1:T(8,128)(2,1)S(1)}, u32[]{:S(2)}, u32[]{:S(2)}) async-start(bf16[1,16,32,256]{3,2,0,1:T(8,128)(2,1)} %fusion.200), calls=%async_computation.10 | async-start | bytes 524288 | tf_op jit(solution)/shard_map/all_to_all | solution.py:60
  311.8 17.6 %all-to-all-done.10 = bf16[1,16,32,256]{3,2,0,1:T(8,128)(2,1)S(1)} async-done(((bf16[1,16,32,256]{3,2,0,1:T(8,128)(2,1)}), bf16[1,16,32,256]{3,2,0,1:T(8,128)(2,1)S(1)}, u32[]{:S(2)}, u32[]{:S(2)}) %all-to-all-start.10) | async-done | bytes 262176 | tf_op jit(solution)/shard_map/all_to_all | solution.py:60
  330.2 22.4 %all_to_all.181 = bf16[16,1,32,256]{3,2,1,0:T(8,128)(2,1)S(1)} all-to-all(bf16[16,1,32,256]{3,2,1,0:T(8,128)(2,1)S(1)} %fusion.46), channel_id=1, replica_groups=mesh['segment'=4,'shard'=16,'stream'=8] {'shard'}, dimensions={0} | all-to-all | bytes 524288 | tf_op jit(solution)/shard_map/all_to_all | solution.py:68
  354.8 4.4 %collective-permute-start.5 = (bf16[1,16,32,256]{3,2,1,0:T(8,128)(2,1)S(1)}, bf16[1,16,32,256]{3,2,1,0:T(8,128)(2,1)S(1)}, u32[]{:S(2)}, u32[]{:S(2)}) collective-permute-start(bf16[1,16,32,256]{3,2,1,0:T(8,128)(2,1)S(1)} %fusion.14), channel_id=1, source_target_pairs={{0,128},{128,256},{256,384},{1,129},{129,257},{257,385},{2,130},{1... | collective-permute-start | bytes 786440 | tf_op jit(solution)/shard_map/ppermute | solution.py:10
  359.2 4.5 %collective-permute-done.5 = bf16[1,16,32,256]{3,2,1,0:T(8,128)(2,1)S(1)} collective-permute-done((bf16[1,16,32,256]{3,2,1,0:T(8,128)(2,1)S(1)}, bf16[1,16,32,256]{3,2,1,0:T(8,128)(2,1)S(1)}, u32[]{:S(2)}, u32[]{:S(2)}) %collective-permute-start.5) | collective-permute-done | bytes 262176 | tf_op jit(solution)/shard_map/ppermute | solution.py:10
  364.0 23.7 %all_to_all.182 = bf16[1,16,32,256]{3,2,0,1:T(8,128)(2,1)S(1)} all-to-all(bf16[1,16,32,256]{3,2,0,1:T(8,128)(2,1)S(1)} %fusion.199), channel_id=1, replica_groups=mesh['segment'=4,'shard'=16,'stream'=8] {'shard'}, dimensions={1} | all-to-all | bytes 524288 | tf_op jit(solution)/shard_map/all_to_all | solution.py:60
  388.5 22.5 %all_to_all.183 = bf16[16,1,32,256]{3,2,1,0:T(8,128)(2,1)S(1)} all-to-all(bf16[16,1,32,256]{3,2,1,0:T(8,128)(2,1)S(1)} %fusion.45), channel_id=1, replica_groups=mesh['segment'=4,'shard'=16,'stream'=8] {'shard'}, dimensions={0} | all-to-all | bytes 524288 | tf_op jit(solution)/shard_map/all_to_all | solution.py:68
  414.8 6.2 %all-to-all-start.14 = ((bf16[4,1,16,32,256]{4,3,2,1,0:T(8,128)(2,1)}), bf16[4,1,16,32,256]{4,3,2,1,0:T(8,128)(2,1)S(1)}, u32[]{:S(2)}, u32[]{:S(2)}) async-start(bf16[4,1,16,32,256]{4,3,2,1,0:T(8,128)(2,1)} %pad_maximum_fusion), calls=%async_computation.14 | async-start | bytes 2097152 | tf_op jit(solution)/shard_map/all_to_all | solution.py:75
  421.7 10.3 %all-to-all-done.14 = bf16[4,1,16,32,256]{4,3,2,1,0:T(8,128)(2,1)S(1)} async-done(((bf16[4,1,16,32,256]{4,3,2,1,0:T(8,128)(2,1)}), bf16[4,1,16,32,256]{4,3,2,1,0:T(8,128)(2,1)S(1)}, u32[]{:S(2)}, u32[]{:S(2)}) %all-to-all-start.14) | async-done | bytes 1048608 | tf_op jit(solution)/shard_map/all_to_all | solution.py:75
  (132 shorter events, 30.0 us)
Async XLA Ops:
  0.6 35.2 %copy-start.1 = (bf16[1,3,256,256]{3,2,1,0:T(8,128)(2,1)S(1)}, bf16[1,3,256,256]{3,2,1,0:T(8,128)(2,1)}, u32[]{:S(2)}) copy-start(bf16[1,3,256,256]{3,2,1,0:T(8,128)(2,1)} %param.7) | copy-start | bytes 1179652
  0.6 35.2 %copy-start.9 = (bf16[1,2,1,32,256]{4,3,2,1,0:T(8,128)(2,1)S(1)}, bf16[1,2,1,32,256]{4,3,2,1,0:T(8,128)(2,1)}, u32[]{:S(2)}) copy-start(bf16[1,2,1,32,256]{4,3,2,1,0:T(8,128)(2,1)} %param.9) | copy-start | bytes 98308
  36.3 24.1 %copy-start = (bf16[1,9,256,256]{3,2,1,0:T(8,128)(2,1)S(1)}, bf16[1,9,256,256]{3,2,1,0:T(8,128)(2,1)}, u32[]{:S(2)}) copy-start(bf16[1,9,256,256]{3,2,1,0:T(8,128)(2,1)} %param.8) | copy-start | bytes 3538948
  61.8 1.2 copy-start.2
  63.1 8.9 %copy-start.10 = (f32[1,256]{1,0:T(1,128)S(1)}, f32[1,256]{1,0:T(1,128)}, u32[]{:S(2)}) copy-start(f32[1,256]{1,0:T(1,128)} %param.6) | copy-start | bytes 3076
  63.3 8.5 %collective-permute-start = (bf16[1,16,32,256]{3,2,1,0:T(8,128)(2,1)S(1)}, bf16[1,16,32,256]{3,2,1,0:T(8,128)(2,1)S(1)}, u32[]{:S(2)}, u32[]{:S(2)}) collective-permute-start(bf16[1,16,32,256]{3,2,1,0:T(8,128)(2,1)S(1)} %fusion.20), channel_id=1, source_target_pairs={{0,128},{128,256},{256,384},{1,129},{129,257},{257,385},{2,130},{1... | collective-permute-start | bytes 786440 | tf_op jit(solution)/shard_map/ppermute | solution.py:10
  72.8 24.6 %all-to-all-start.2 = ((bf16[1,16,32,256]{3,2,0,1:T(8,128)(2,1)}), bf16[1,16,32,256]{3,2,0,1:T(8,128)(2,1)S(1)}, u32[]{:S(2)}, u32[]{:S(2)}) async-start(bf16[1,16,32,256]{3,2,0,1:T(8,128)(2,1)} %fusion.204), calls=%async_computation.2 | async-start | bytes 524288 | tf_op jit(solution)/shard_map/all_to_all | solution.py:60
  123.7 8.2 %collective-permute-start.1 = (bf16[1,16,32,256]{3,2,1,0:T(8,128)(2,1)S(1)}, bf16[1,16,32,256]{3,2,1,0:T(8,128)(2,1)S(1)}, u32[]{:S(2)}, u32[]{:S(2)}) collective-permute-start(bf16[1,16,32,256]{3,2,1,0:T(8,128)(2,1)S(1)} %fusion.18), channel_id=1, source_target_pairs={{0,128},{128,256},{256,384},{1,129},{129,257},{257,385},{2,130},{1... | collective-permute-start | bytes 786440 | tf_op jit(solution)/shard_map/ppermute | solution.py:10
  180.3 8.9 %collective-permute-start.2 = (bf16[1,16,32,256]{3,2,1,0:T(8,128)(2,1)S(1)}, bf16[1,16,32,256]{3,2,1,0:T(8,128)(2,1)S(1)}, u32[]{:S(2)}, u32[]{:S(2)}) collective-permute-start(bf16[1,16,32,256]{3,2,1,0:T(8,128)(2,1)S(1)} %fusion.17), channel_id=1, source_target_pairs={{0,128},{128,256},{256,384},{1,129},{129,257},{257,385},{2,130},{1... | collective-permute-start | bytes 786440 | tf_op jit(solution)/shard_map/ppermute | solution.py:10
  189.4 0.7 copy-start.3
  191.0 23.9 %all-to-all-start.6 = ((bf16[1,16,32,256]{3,2,0,1:T(8,128)(2,1)}), bf16[1,16,32,256]{3,2,0,1:T(8,128)(2,1)S(1)}, u32[]{:S(2)}, u32[]{:S(2)}) async-start(bf16[1,16,32,256]{3,2,0,1:T(8,128)(2,1)} %fusion.202), calls=%async_computation.6 | async-start | bytes 524288 | tf_op jit(solution)/shard_map/all_to_all | solution.py:60
  239.6 1.0 copy-start.4
  240.8 30.9 %copy-start.5 = (bf16[1,16,32,256]{3,2,1,0:T(8,128)(2,1)}, bf16[1,16,32,256]{3,2,1,0:T(8,128)(2,1)S(1)}, u32[]{:S(2)}) copy-start(bf16[1,16,32,256]{3,2,1,0:T(8,128)(2,1)S(1)} %fusion.16) | copy-start | bytes 786436
  240.8 8.4 %collective-permute-start.3 = (bf16[1,16,32,256]{3,2,1,0:T(8,128)(2,1)S(1)}, bf16[1,16,32,256]{3,2,1,0:T(8,128)(2,1)S(1)}, u32[]{:S(2)}, u32[]{:S(2)}) collective-permute-start(bf16[1,16,32,256]{3,2,1,0:T(8,128)(2,1)S(1)} %fusion.16), channel_id=1, source_target_pairs={{0,128},{128,256},{256,384},{1,129},{129,257},{257,385},{2,130},{1... | collective-permute-start | bytes 786440 | tf_op jit(solution)/shard_map/ppermute | solution.py:10
  296.4 9.4 %copy-start.7 = (bf16[1,16,32,256]{3,2,1,0:T(8,128)(2,1)}, bf16[1,16,32,256]{3,2,1,0:T(8,128)(2,1)S(1)}, u32[]{:S(2)}) copy-start(bf16[1,16,32,256]{3,2,1,0:T(8,128)(2,1)S(1)} %fusion.15) | copy-start | bytes 786436
  296.4 8.4 %collective-permute-start.4 = (bf16[1,16,32,256]{3,2,1,0:T(8,128)(2,1)S(1)}, bf16[1,16,32,256]{3,2,1,0:T(8,128)(2,1)S(1)}, u32[]{:S(2)}, u32[]{:S(2)}) collective-permute-start(bf16[1,16,32,256]{3,2,1,0:T(8,128)(2,1)S(1)} %fusion.15), channel_id=1, source_target_pairs={{0,128},{128,256},{256,384},{1,129},{129,257},{257,385},{2,130},{1... | collective-permute-start | bytes 786440 | tf_op jit(solution)/shard_map/ppermute | solution.py:10
  305.8 23.6 %all-to-all-start.10 = ((bf16[1,16,32,256]{3,2,0,1:T(8,128)(2,1)}), bf16[1,16,32,256]{3,2,0,1:T(8,128)(2,1)S(1)}, u32[]{:S(2)}, u32[]{:S(2)}) async-start(bf16[1,16,32,256]{3,2,0,1:T(8,128)(2,1)} %fusion.200), calls=%async_computation.10 | async-start | bytes 524288 | tf_op jit(solution)/shard_map/all_to_all | solution.py:60
  354.8 8.9 %collective-permute-start.5 = (bf16[1,16,32,256]{3,2,1,0:T(8,128)(2,1)S(1)}, bf16[1,16,32,256]{3,2,1,0:T(8,128)(2,1)S(1)}, u32[]{:S(2)}, u32[]{:S(2)}) collective-permute-start(bf16[1,16,32,256]{3,2,1,0:T(8,128)(2,1)S(1)} %fusion.14), channel_id=1, source_target_pairs={{0,128},{128,256},{256,384},{1,129},{129,257},{257,385},{2,130},{1... | collective-permute-start | bytes 786440 | tf_op jit(solution)/shard_map/ppermute | solution.py:10
  412.6 1.0 copy-start.6
  412.7 1.0 copy-start.8
  414.8 17.1 %all-to-all-start.14 = ((bf16[4,1,16,32,256]{4,3,2,1,0:T(8,128)(2,1)}), bf16[4,1,16,32,256]{4,3,2,1,0:T(8,128)(2,1)S(1)}, u32[]{:S(2)}, u32[]{:S(2)}) async-start(bf16[4,1,16,32,256]{4,3,2,1,0:T(8,128)(2,1)} %pad_maximum_fusion), calls=%async_computation.14 | async-start | bytes 2097152 | tf_op jit(solution)/shard_map/all_to_all | solution.py:75
where the time goes:
time: 434 us; the launch traced here: 433 us
  blocking collectives  260 us (60%)
  waiting for transfers between devices  88.7 us (20%)
  starting transfers between devices  51.3 us (12%)
  matrix products  20 us (5%)
  other arithmetic  7.9 us (2%)
    all_to_all x7, blocking collectives, body(): lax.all_to_all(row_hidden, 'shard', split_axis=0, concat_axis=1, tiled=True)  159 us
    all_to_all x4, blocking collectives, body(): lax.all_to_all(normed, 'shard', split_axis=1, concat_axis=0, tiled=True)  101 us
    all_to_all x3, waiting for transfers between devices, body(): lax.all_to_all(normed, 'shard', split_axis=1, concat_axis=0, tiled=True)  52.9 us
    ppermute x6, starting transfers between devices, shifted(): return lax.ppermute(block, axis, route)  25.8 us
    ppermute x6, waiting for transfers between devices, shifted(): return lax.ppermute(block, axis, route)  25.6 us
    dot_general x84, matrix products, project(): jnp.dot(frames_in.reshape(-1, channels), matrix, preferred_element_type=j...  20 us
    all_to_all x3, starting transfers between devices, body(): lax.all_to_all(normed, 'shard', split_axis=1, concat_axis=0, tiled=True)  19.2 us
    all_to_all x1, waiting for transfers between devices, body(): lax.all_to_all(stacked, 'segment', split_axis=0, concat_axis=0, tiled=True)  10.3 us
  transfers between devices with their start and end apart: 10, of which 10 were waited for; matrix products, arithmetic and copies ran while one was open for 0% of the time, Pallas kernels for 0%

commit v1 on v0

--- a/solution.py
+++ b/solution.py
@@ -57,7 +57,12 @@
         current = jnp.where(segment_pos == 0, fresh, arriving)
         active = jnp.logical_and(turn - segment_pos >= 0, turn - segment_pos < block_count)
         normed = normalize(current, gain_row)
-        by_rows = lax.all_to_all(normed, "shard", split_axis=1, concat_axis=0, tiled=True)
+        by_rows = jnp.concatenate(
+            lax.all_to_all(
+                jnp.stack(jnp.split(normed, lax.axis_size("shard"), 1), axis=0), "shard", 0, 0
+            ),
+            axis=0,
+        )
         frame_count = by_rows.shape[0]
         extended = jnp.concatenate([earlier, by_rows], axis=0)
         mixed = project(extended[0:frame_count], taps[0])

time: 434 us -> 463 us (1.067)
  the two profiles are of different devices: /device:TPU:38 before, /device:TPU:32 now
where the time goes in v1:
time: 463 us; the launch traced here: 462 us
  blocking collectives  261 us (56%)
  waiting for transfers between devices  92 us (20%)
  starting transfers between devices  48.5 us (10%)
  local copies, waits for them, and re-layouts  32.5 us (7%)
  matrix products  20 us (4%)
  other arithmetic  5.78 us (1%)
    all_to_all x7, blocking collectives, body(): lax.all_to_all(row_hidden, 'shard', split_axis=0, concat_axis=1, tiled=True)  159 us
    all_to_all x4, blocking collectives, body(): lax.all_to_all(jnp.stack(jnp.split(normed, lax.axis_size('shard'), 1), ax...  102 us
    all_to_all x3, waiting for transfers between devices, body(): lax.all_to_all(jnp.stack(jnp.split(normed, lax.axis_size('shard'), 1), ax...  52.7 us
    unnamed x127, local copies, waits for them, and re-layouts  30 us
    ppermute x6, waiting for transfers between devices, shifted(): return lax.ppermute(block, axis, route)  26.1 us
    ppermute x6, starting transfers between devices, shifted(): return lax.ppermute(block, axis, route)  25.5 us
    dot_general x84, matrix products, project(): jnp.dot(frames_in.reshape(-1, channels), matrix, preferred_element_type=j...  20 us
    all_to_all x3, starting transfers between devices, body(): lax.all_to_all(jnp.stack(jnp.split(normed, lax.axis_size('shard'), 1), ax...  19.2 us
  transfers between devices with their start and end apart: 10, of which 10 were waited for; matrix products, arithmetic and copies ran while one was open for 0% of the time, Pallas kernels for 0%

profile of v1, /device:TPU:32, one launch (start us, length us, event | category | flops | bytes accessed | tf_op | source)
XLA Modules:
  0.0 461.6 jit_solution(8077085484896885736)
XLA Ops:
  0.7 1.1 fusion.24
  3.1 32.9 %all_to_all.124 = bf16[16,1,1,32,256]{4,3,2,1,0:T(8,128)(2,1)S(1)} all-to-all(bf16[16,1,1,32,256]{4,3,2,1,0:T(8,128)(2,1)S(1)} %constant_dynamic-update-slice_fusion), channel_id=1, replica_groups=mesh['segment'=4,'shard'=16,'stream'=8] {'shard'}, dimensions={0} | all-to-all | bytes 524288 | tf_op jit(solution)/shard_map/all_to_all | solution.py:61
  36.8 23.7 %all_to_all.125 = bf16[16,1,32,256]{3,2,1,0:T(8,128)(2,1)S(1)} all-to-all(bf16[16,1,32,256]{3,2,1,0:T(8,128)(2,1)S(1)} %fusion.51), channel_id=1, replica_groups=mesh['segment'=4,'shard'=16,'stream'=8] {'shard'}, dimensions={0} | all-to-all | bytes 524288 | tf_op jit(solution)/shard_map/all_to_all | solution.py:73
  63.5 3.5 collective-permute-start
  67.0 5.0 %collective-permute-done = bf16[1,16,32,256]{3,2,1,0:T(8,128)(2,1)S(1)} collective-permute-done((bf16[1,16,32,256]{3,2,1,0:T(8,128)(2,1)S(1)}, bf16[1,16,32,256]{3,2,1,0:T(8,128)(2,1)S(1)}, u32[]{:S(2)}, u32[]{:S(2)}) %collective-permute-start) | collective-permute-done | bytes 262176 | tf_op jit(solution)/shard_map/ppermute | solution.py:10
  82.0 7.0 %all-to-all-start.2 = ((bf16[16,1,1,32,256]{4,3,2,1,0:T(8,128)(2,1)}), bf16[16,1,1,32,256]{4,3,2,1,0:T(8,128)(2,1)S(1)}, u32[]{:S(2)}, u32[]{:S(2)}) async-start(bf16[16,1,1,32,256]{4,3,2,1,0:T(8,128)(2,1)} %constant_dynamic-update-slice_fusion.16), calls=%async_computation.2 | async-start | bytes 524288 | tf_op jit(solution)/shard_map/all_to_all | solution.py:61
  89.0 17.6 %all-to-all-done.2 = bf16[16,1,1,32,256]{4,3,2,1,0:T(8,128)(2,1)S(1)} async-done(((bf16[16,1,1,32,256]{4,3,2,1,0:T(8,128)(2,1)}), bf16[16,1,1,32,256]{4,3,2,1,0:T(8,128)(2,1)S(1)}, u32[]{:S(2)}, u32[]{:S(2)}) %all-to-all-start.2) | async-done | bytes 262176 | tf_op jit(solution)/shard_map/all_to_all | solution.py:61
  107.4 23.0 %all_to_all.126 = bf16[16,1,32,256]{3,2,1,0:T(8,128)(2,1)S(1)} all-to-all(bf16[16,1,32,256]{3,2,1,0:T(8,128)(2,1)S(1)} %fusion.50), channel_id=1, replica_groups=mesh['segment'=4,'shard'=16,'stream'=8] {'shard'}, dimensions={0} | all-to-all | bytes 524288 | tf_op jit(solution)/shard_map/all_to_all | solution.py:73
  132.5 4.4 collective-permute-start.1
  136.9 4.4 collective-permute-done.1
  141.8 23.4 %all_to_all.127 = bf16[16,1,1,32,256]{4,3,2,1,0:T(8,128)(2,1)S(1)} all-to-all(bf16[16,1,1,32,256]{4,3,2,1,0:T(8,128)(2,1)S(1)} %constant_dynamic-update-slice_fusion.32), channel_id=1, replica_groups=mesh['segment'=4,'shard'=16,'stream'=8] {'shard'}, dimensions={0} | all-to-all | bytes 524288 | tf_op jit(solution)/shard_map/all_to_all | solution.py:61
  166.0 22.4 %all_to_all.128 = bf16[16,1,32,256]{3,2,1,0:T(8,128)(2,1)S(1)} all-to-all(bf16[16,1,32,256]{3,2,1,0:T(8,128)(2,1)S(1)} %fusion.49), channel_id=1, replica_groups=mesh['segment'=4,'shard'=16,'stream'=8] {'shard'}, dimensions={0} | all-to-all | bytes 524288 | tf_op jit(solution)/shard_map/all_to_all | solution.py:73
  190.6 4.4 collective-permute-start.2
  195.0 4.5 collective-permute-done.2
  210.2 6.3 %all-to-all-start.6 = ((bf16[16,1,1,32,256]{4,3,2,1,0:T(8,128)(2,1)}), bf16[16,1,1,32,256]{4,3,2,1,0:T(8,128)(2,1)S(1)}, u32[]{:S(2)}, u32[]{:S(2)}) async-start(bf16[16,1,1,32,256]{4,3,2,1,0:T(8,128)(2,1)} %constant_dynamic-update-slice_fusion.48), calls=%async_computation.6 | async-start | bytes 524288 | tf_op jit(solution)/shard_map/all_to_all | solution.py:61
  216.6 17.7 %all-to-all-done.6 = bf16[16,1,1,32,256]{4,3,2,1,0:T(8,128)(2,1)S(1)} async-done(((bf16[16,1,1,32,256]{4,3,2,1,0:T(8,128)(2,1)}), bf16[16,1,1,32,256]{4,3,2,1,0:T(8,128)(2,1)S(1)}, u32[]{:S(2)}, u32[]{:S(2)}) %all-to-all-start.6) | async-done | bytes 262176 | tf_op jit(solution)/shard_map/all_to_all | solution.py:61
  235.0 22.5 %all_to_all.129 = bf16[16,1,32,256]{3,2,1,0:T(8,128)(2,1)S(1)} all-to-all(bf16[16,1,32,256]{3,2,1,0:T(8,128)(2,1)S(1)} %fusion.48), channel_id=1, replica_groups=mesh['segment'=4,'shard'=16,'stream'=8] {'shard'}, dimensions={0} | all-to-all | bytes 524288 | tf_op jit(solution)/shard_map/all_to_all | solution.py:73
  260.2 4.4 collective-permute-start.3
  264.6 3.9 collective-permute-done.3
  268.9 21.7 %all_to_all.130 = bf16[16,1,1,32,256]{4,3,2,1,0:T(8,128)(2,1)S(1)} all-to-all(bf16[16,1,1,32,256]{4,3,2,1,0:T(8,128)(2,1)S(1)} %constant_dynamic-update-slice_fusion.64), channel_id=1, replica_groups=mesh['segment'=4,'shard'=16,'stream'=8] {'shard'}, dimensions={0} | all-to-all | bytes 524288 | tf_op jit(solution)/shard_map/all_to_all | solution.py:61
  291.4 22.3 %all_to_all.131 = bf16[16,1,32,256]{3,2,1,0:T(8,128)(2,1)S(1)} all-to-all(bf16[16,1,32,256]{3,2,1,0:T(8,128)(2,1)S(1)} %fusion.47), channel_id=1, replica_groups=mesh['segment'=4,'shard'=16,'stream'=8] {'shard'}, dimensions={0} | all-to-all | bytes 524288 | tf_op jit(solution)/shard_map/all_to_all | solution.py:73
  315.8 4.4 collective-permute-start.4
  320.3 3.9 collective-permute-done.4
  334.1 5.9 %all-to-all-start.10 = ((bf16[16,1,1,32,256]{4,3,2,1,0:T(8,128)(2,1)}), bf16[16,1,1,32,256]{4,3,2,1,0:T(8,128)(2,1)S(1)}, u32[]{:S(2)}, u32[]{:S(2)}) async-start(bf16[16,1,1,32,256]{4,3,2,1,0:T(8,128)(2,1)} %constant_dynamic-update-slice_fusion.80), calls=%async_computation.10 | async-start | bytes 524288 | tf_op jit(solution)/shard_map/all_to_all | solution.py:61
  340.0 17.5 %all-to-all-done.10 = bf16[16,1,1,32,256]{4,3,2,1,0:T(8,128)(2,1)S(1)} async-done(((bf16[16,1,1,32,256]{4,3,2,1,0:T(8,128)(2,1)}), bf16[16,1,1,32,256]{4,3,2,1,0:T(8,128)(2,1)S(1)}, u32[]{:S(2)}, u32[]{:S(2)}) %all-to-all-start.10) | async-done | bytes 262176 | tf_op jit(solution)/shard_map/all_to_all | solution.py:61
  358.3 22.4 %all_to_all.132 = bf16[16,1,32,256]{3,2,1,0:T(8,128)(2,1)S(1)} all-to-all(bf16[16,1,32,256]{3,2,1,0:T(8,128)(2,1)S(1)} %fusion.46), channel_id=1, replica_groups=mesh['segment'=4,'shard'=16,'stream'=8] {'shard'}, dimensions={0} | all-to-all | bytes 524288 | tf_op jit(solution)/shard_map/all_to_all | solution.py:73
  382.9 4.4 collective-permute-start.5
  387.3 4.5 collective-permute-done.5
  392.3 23.8 %all_to_all.133 = bf16[16,1,1,32,256]{4,3,2,1,0:T(8,128)(2,1)S(1)} all-to-all(bf16[16,1,1,32,256]{4,3,2,1,0:T(8,128)(2,1)S(1)} %constant_dynamic-update-slice_fusion.96), channel_id=1, replica_groups=mesh['segment'=4,'shard'=16,'stream'=8] {'shard'}, dimensions={0} | all-to-all | bytes 524288 | tf_op jit(solution)/shard_map/all_to_all | solution.py:61
  416.9 22.5 %all_to_all.134 = bf16[16,1,32,256]{3,2,1,0:T(8,128)(2,1)S(1)} all-to-all(bf16[16,1,32,256]{3,2,1,0:T(8,128)(2,1)S(1)} %fusion.45), channel_id=1, replica_groups=mesh['segment'=4,'shard'=16,'stream'=8] {'shard'}, dimensions={0} | all-to-all | bytes 524288 | tf_op jit(solution)/shard_map/all_to_all | solution.py:73
  443.2 3.7 all-to-all-start.14
  447.6 13.3 %all-to-all-done.14 = bf16[4,1,16,32,256]{4,3,2,1,0:T(8,128)(2,1)S(1)} async-done(((bf16[4,1,16,32,256]{4,3,2,1,0:T(8,128)(2,1)}), bf16[4,1,16,32,256]{4,3,2,1,0:T(8,128)(2,1)S(1)}, u32[]{:S(2)}, u32[]{:S(2)}) %all-to-all-start.14) | async-done | bytes 1048608 | tf_op jit(solution)/shard_map/all_to_all | solution.py:80
  (244 shorter events, 57.2 us)
Async XLA Ops:
  0.6 35.4 %copy-start.1 = (bf16[1,3,256,256]{3,2,1,0:T(8,128)(2,1)S(1)}, bf16[1,3,256,256]{3,2,1,0:T(8,128)(2,1)}, u32[]{:S(2)}) copy-start(bf16[1,3,256,256]{3,2,1,0:T(8,128)(2,1)} %param.7) | copy-start | bytes 1179652
  0.6 35.4 %copy-start.9 = (bf16[1,2,1,32,256]{4,3,2,1,0:T(8,128)(2,1)S(1)}, bf16[1,2,1,32,256]{4,3,2,1,0:T(8,128)(2,1)}, u32[]{:S(2)}) copy-start(bf16[1,2,1,32,256]{4,3,2,1,0:T(8,128)(2,1)} %param.9) | copy-start | bytes 98308
  36.5 24.1 %copy-start = (bf16[1,9,256,256]{3,2,1,0:T(8,128)(2,1)S(1)}, bf16[1,9,256,256]{3,2,1,0:T(8,128)(2,1)}, u32[]{:S(2)}) copy-start(bf16[1,9,256,256]{3,2,1,0:T(8,128)(2,1)} %param.8) | copy-start | bytes 3538948
  62.0 1.2 copy-start.2
  63.2 8.9 %copy-start.10 = (f32[1,256]{1,0:T(1,128)S(1)}, f32[1,256]{1,0:T(1,128)}, u32[]{:S(2)}) copy-start(f32[1,256]{1,0:T(1,128)} %param.6) | copy-start | bytes 3076
  63.5 8.5 %collective-permute-start = (bf16[1,16,32,256]{3,2,1,0:T(8,128)(2,1)S(1)}, bf16[1,16,32,256]{3,2,1,0:T(8,128)(2,1)S(1)}, u32[]{:S(2)}, u32[]{:S(2)}) collective-permute-start(bf16[1,16,32,256]{3,2,1,0:T(8,128)(2,1)S(1)} %fusion.20), channel_id=1, source_target_pairs={{0,128},{128,256},{256,384},{1,129},{129,257},{257,385},{2,130},{1... | collective-permute-start | bytes 786440 | tf_op jit(solution)/shard_map/ppermute | solution.py:10
  82.0 24.5 %all-to-all-start.2 = ((bf16[16,1,1,32,256]{4,3,2,1,0:T(8,128)(2,1)}), bf16[16,1,1,32,256]{4,3,2,1,0:T(8,128)(2,1)S(1)}, u32[]{:S(2)}, u32[]{:S(2)}) async-start(bf16[16,1,1,32,256]{4,3,2,1,0:T(8,128)(2,1)} %constant_dynamic-update-slice_fusion.16), calls=%async_computation.2 | async-start | bytes 524288 | tf_op jit(solution)/shard_map/all_to_all | solution.py:61
  132.5 8.8 %collective-permute-start.1 = (bf16[1,16,32,256]{3,2,1,0:T(8,128)(2,1)S(1)}, bf16[1,16,32,256]{3,2,1,0:T(8,128)(2,1)S(1)}, u32[]{:S(2)}, u32[]{:S(2)}) collective-permute-start(bf16[1,16,32,256]{3,2,1,0:T(8,128)(2,1)S(1)} %fusion.18), channel_id=1, source_target_pairs={{0,128},{128,256},{256,384},{1,129},{129,257},{257,385},{2,130},{1... | collective-permute-start | bytes 786440 | tf_op jit(solution)/shard_map/ppermute | solution.py:10
  190.6 8.9 %collective-permute-start.2 = (bf16[1,16,32,256]{3,2,1,0:T(8,128)(2,1)S(1)}, bf16[1,16,32,256]{3,2,1,0:T(8,128)(2,1)S(1)}, u32[]{:S(2)}, u32[]{:S(2)}) collective-permute-start(bf16[1,16,32,256]{3,2,1,0:T(8,128)(2,1)S(1)} %fusion.17), channel_id=1, source_target_pairs={{0,128},{128,256},{256,384},{1,129},{129,257},{257,385},{2,130},{1... | collective-permute-start | bytes 786440 | tf_op jit(solution)/shard_map/ppermute | solution.py:10
  199.7 0.7 copy-start.3
  210.2 24.0 %all-to-all-start.6 = ((bf16[16,1,1,32,256]{4,3,2,1,0:T(8,128)(2,1)}), bf16[16,1,1,32,256]{4,3,2,1,0:T(8,128)(2,1)S(1)}, u32[]{:S(2)}, u32[]{:S(2)}) async-start(bf16[16,1,1,32,256]{4,3,2,1,0:T(8,128)(2,1)} %constant_dynamic-update-slice_fusion.48), calls=%async_computation.6 | async-start | bytes 524288 | tf_op jit(solution)/shard_map/all_to_all | solution.py:61
  259.0 1.0 copy-start.4
  260.2 30.6 %copy-start.5 = (bf16[1,16,32,256]{3,2,1,0:T(8,128)(2,1)}, bf16[1,16,32,256]{3,2,1,0:T(8,128)(2,1)S(1)}, u32[]{:S(2)}) copy-start(bf16[1,16,32,256]{3,2,1,0:T(8,128)(2,1)S(1)} %fusion.16) | copy-start | bytes 786436
  260.2 8.2 %collective-permute-start.3 = (bf16[1,16,32,256]{3,2,1,0:T(8,128)(2,1)S(1)}, bf16[1,16,32,256]{3,2,1,0:T(8,128)(2,1)S(1)}, u32[]{:S(2)}, u32[]{:S(2)}) collective-permute-start(bf16[1,16,32,256]{3,2,1,0:T(8,128)(2,1)S(1)} %fusion.16), channel_id=1, source_target_pairs={{0,128},{128,256},{256,384},{1,129},{129,257},{257,385},{2,130},{1... | collective-permute-start | bytes 786440 | tf_op jit(solution)/shard_map/ppermute | solution.py:10
  315.8 8.4 %copy-start.7 = (bf16[1,16,32,256]{3,2,1,0:T(8,128)(2,1)}, bf16[1,16,32,256]{3,2,1,0:T(8,128)(2,1)S(1)}, u32[]{:S(2)}) copy-start(bf16[1,16,32,256]{3,2,1,0:T(8,128)(2,1)S(1)} %fusion.15) | copy-start | bytes 786436
  315.8 8.3 %collective-permute-start.4 = (bf16[1,16,32,256]{3,2,1,0:T(8,128)(2,1)S(1)}, bf16[1,16,32,256]{3,2,1,0:T(8,128)(2,1)S(1)}, u32[]{:S(2)}, u32[]{:S(2)}) collective-permute-start(bf16[1,16,32,256]{3,2,1,0:T(8,128)(2,1)S(1)} %fusion.15), channel_id=1, source_target_pairs={{0,128},{128,256},{256,384},{1,129},{129,257},{257,385},{2,130},{1... | collective-permute-start | bytes 786440 | tf_op jit(solution)/shard_map/ppermute | solution.py:10
  334.1 23.4 %all-to-all-start.10 = ((bf16[16,1,1,32,256]{4,3,2,1,0:T(8,128)(2,1)}), bf16[16,1,1,32,256]{4,3,2,1,0:T(8,128)(2,1)S(1)}, u32[]{:S(2)}, u32[]{:S(2)}) async-start(bf16[16,1,1,32,256]{4,3,2,1,0:T(8,128)(2,1)} %constant_dynamic-update-slice_fusion.80), calls=%async_computation.10 | async-start | bytes 524288 | tf_op jit(solution)/shard_map/all_to_all | solution.py:61
  382.9 8.9 %collective-permute-start.5 = (bf16[1,16,32,256]{3,2,1,0:T(8,128)(2,1)S(1)}, bf16[1,16,32,256]{3,2,1,0:T(8,128)(2,1)S(1)}, u32[]{:S(2)}, u32[]{:S(2)}) collective-permute-start(bf16[1,16,32,256]{3,2,1,0:T(8,128)(2,1)S(1)} %fusion.14), channel_id=1, source_target_pairs={{0,128},{128,256},{256,384},{1,129},{129,257},{257,385},{2,130},{1... | collective-permute-start | bytes 786440 | tf_op jit(solution)/shard_map/ppermute | solution.py:10
  441.1 1.0 copy-start.6
  441.1 1.0 copy-start.8
  443.2 17.6 %all-to-all-start.14 = ((bf16[4,1,16,32,256]{4,3,2,1,0:T(8,128)(2,1)}), bf16[4,1,16,32,256]{4,3,2,1,0:T(8,128)(2,1)S(1)}, u32[]{:S(2)}, u32[]{:S(2)}) async-start(bf16[4,1,16,32,256]{4,3,2,1,0:T(8,128)(2,1)} %pad_maximum_fusion), calls=%async_computation.14 | async-start | bytes 2097152 | tf_op jit(solution)/shard_map/all_to_all | solution.py:80
